TPU v7x, 128 devices: a whole 4x4x4 slice. The times are simulated.
128 devices in a mesh: src: 32 (over y, z, core), rcv: 4 (over x).
Axes of the slice: x: 4, y: 4, z: 4, core: 2. Of those that a mesh axis runs over, the one named last changes fastest.
Arguments:
- traces: bfloat16 [262144, 2048], P(('src', 'rcv'))
- trace_source: int32 [262144], P(('src', 'rcv')), may hold values from 0 to 255, as said below
- trace_offset: int32 [262144], P(('src', 'rcv')), may hold values from 0 to 63
- trace_slot: int32 [262144], P(('src', 'rcv')), may hold values from 0 to 1023, as said below
- request_list: int32 [128, 128, 8], P(('src', 'rcv')), may hold values from 0 to 63, as said below
- source_terms: float32 [256, 1024], P('src'), may hold values from -3 to 3
- receiver_terms: float32 [8192, 1024], P(('src', 'rcv')), may hold values from -3 to 3
- offset_terms: float32 [64, 1024], replicated, may hold values from -3 to 3
Outputs:
- source_new: float32 [256, 1024], P('src')
- receiver_new: float32 [8192, 1024], P(('src', 'rcv'))
- offset_new: float32 [64, 1024], replicated
Inputs may be any that keep to these rules, and one draw needn't show every extreme that they name: `trace_source`: trace t's source is one of the 8 sources of the src index that holds t. `request_list`: within one device's list for one owner the 8 entries are distinct. `trace_slot`: a slot names an owner and a position in the holding device's own request list.
All inputs are finite; a program needn't handle non-finite values.
Results may differ from a plain program's by a relative error of at most 0.0023.
Values sent between devices are 32-bit elements; how exact they have to be, the bound alone decides.
A program may use at most 128 MiB of HBM per device.

v0:
```python
import math
import jax
import jax.numpy as jnp
from jax import lax
from jax.sharding import PartitionSpec as P


def dft_table(samples):
    freq = samples // 2
    index_n = lax.broadcasted_iota(jnp.int32, (samples, freq), 0)
    index_f = lax.broadcasted_iota(jnp.int32, (samples, freq), 1)
    phase = (index_n * index_f % samples).astype(jnp.float32) * (2.0 * math.pi / samples)
    taper = 0.5 - 0.5 * jnp.cos((index_n.astype(jnp.float32) + 0.5) * (2.0 * math.pi / samples))
    scaled = taper / math.sqrt(samples)
    return jnp.concatenate([scaled * jnp.cos(phase), -scaled * jnp.sin(phase)], axis=1).astype(
        jnp.bfloat16
    )


def collect(one_hot, residual):
    upper = residual.astype(jnp.bfloat16)
    lower = (residual - upper.astype(jnp.float32)).astype(jnp.bfloat16)
    dims = (((0,), (0,)), ((), ()))
    first = lax.dot_general(one_hot, upper, dims, preferred_element_type=jnp.float32)
    second = lax.dot_general(one_hot, lower, dims, preferred_element_type=jnp.float32)
    return first + second


def local(
    traces,
    trace_source,
    trace_offset,
    trace_slot,
    request_list,
    source_terms,
    receiver_terms,
    offset_terms,
):
    peers = lax.axis_size(("src", "rcv"))
    slots = request_list.shape[2]
    freq = receiver_terms.shape[1]
    owned = receiver_terms.shape[0]
    requests = request_list.reshape(peers, slots)
    asked = lax.all_to_all(requests, ("src", "rcv"), split_axis=0, concat_axis=0, tiled=True)
    served = receiver_terms[asked.reshape(-1)].reshape(peers, slots, freq)
    fetched = lax.all_to_all(
        served, ("src", "rcv"), split_axis=0, concat_axis=0, tiled=True
    ).reshape(peers * slots, freq)
    table = dft_table(traces.shape[1])
    spectra = jnp.dot(traces, table, preferred_element_type=jnp.float32)
    real_part = spectra[:, :freq]
    imag_part = spectra[:, freq:]
    logamp = 0.5 * jnp.log(real_part * real_part + imag_part * imag_part + 0.01)
    num_src = source_terms.shape[0]
    num_off = offset_terms.shape[0]
    src_local = trace_source - lax.axis_index("src") * num_src
    residual = logamp - source_terms[src_local] - fetched[trace_slot] - offset_terms[trace_offset]
    ones = jnp.ones((traces.shape[0],), jnp.float32)
    rcv_part = jax.ops.segment_sum(residual, trace_slot, num_segments=peers * slots).reshape(
        peers, slots, freq
    )
    rcv_cnt = jax.ops.segment_sum(ones, trace_slot, num_segments=peers * slots).reshape(
        peers, slots
    )
    got_part, got_cnt = (
        lax.all_to_all(rcv_part, ("src", "rcv"), split_axis=0, concat_axis=0, tiled=True),
        lax.all_to_all(rcv_cnt, ("src", "rcv"), split_axis=0, concat_axis=0, tiled=True),
    )
    flat_asked = asked.reshape(-1)
    rcv_grad = jax.ops.segment_sum(
        got_part.reshape(peers * slots, freq), flat_asked, num_segments=owned
    )
    rcv_total = jax.ops.segment_sum(got_cnt.reshape(peers * slots), flat_asked, num_segments=owned)
    receiver_new = receiver_terms + rcv_grad / (rcv_total + 1.0)[:, None]
    columns = jnp.arange(num_src + num_off, dtype=jnp.int32)[None, :]
    both_hot = (
        (src_local[:, None] == columns) | ((trace_offset + num_src)[:, None] == columns)
    ).astype(jnp.bfloat16)
    joint = collect(both_hot, residual)
    joint_cnt = jnp.sum(both_hot.astype(jnp.float32), axis=0)
    src_part = joint[:num_src]
    off_part = joint[num_src:]
    src_cnt = joint_cnt[:num_src]
    off_cnt = joint_cnt[num_src:]
    src_sum, src_tot = lax.psum((src_part, src_cnt), "rcv")
    off_sum, off_tot = lax.psum((off_part, off_cnt), ("src", "rcv"))
    source_new = source_terms + src_sum / (src_tot + 1.0)[:, None]
    offset_new = offset_terms + off_sum / (off_tot + 1.0)[:, None]
    return (source_new, receiver_new, offset_new)


def solution(mesh):
    return jax.shard_map(
        local,
        mesh=mesh,
        in_specs=(
            P(("src", "rcv"), None),
            P(("src", "rcv")),
            P(("src", "rcv")),
            P(("src", "rcv")),
            P(("src", "rcv"), None, None),
            P("src", None),
            P(("src", "rcv"), None),
            P(),
        ),
        out_specs=(P("src", None), P(("src", "rcv"), None), P()),
        check_vma=False,
    )
```

profile of v0, /device:TPU:1, one launch (start us, length us, event | category | flops | bytes accessed | tf_op | source)
XLA Modules:
  0.0 526.6 jit_solution(12145871328240511562)
XLA Ops:
  7.2 0.0 copy-start
  7.2 1.4 copy.27
  8.6 11.5 %all-to-all-start = ((s32[128,1,8]{2,1,0:T(1,128)}), s32[128,1,8]{2,1,0:T(1,128)S(1)}, u32[]{:S(2)}, u32[]{:S(2)}) async-start(s32[128,1,8]{2,1,0:T(1,128)} %bitcast.1), calls=%async_computation | async-start | bytes 131072 | tf_op jit(solution)/shard_map/all_to_all | solution.py:44
  20.1 0.1 fusion.39
  20.2 0.7 fusion.37
  20.9 0.7 fusion.36
  21.6 0.1 subtract_multiply_fusion
  21.7 14.8 %scatter_custom_fusion.2 = f32[1024]{0:T(1024)S(1)} fusion(s32[2048]{0:T(1024)} %param.11, f32[2048]{0:T(1024)S(1)} %broadcast.70, f32[]{:T(128)} %constant.12.clone.1), kind=kCustom, calls=%fused_computation.67 | custom fusion | flops 2048 | bytes 4608 | tf_op jit(solution)/shard_map/scatter-add | solution.py:62
  36.5 0.7 all_to_all.22
  37.2 0.0 copy-done
  37.2 9.8 %gather_fusion = f32[2048,1024]{1,0:T(8,128)} fusion(f32[8,1024]{1,0:T(8,128)S(1)} %copy-done, s32[2048]{0:T(1024)S(1)} %get-tuple-element.5), kind=kCustom, calls=%fused_computation | custom fusion | bytes 16785408 | tf_op jit(solution)/shard_map/gather | solution.py:57
  47.0 0.0 copy-start.1
  47.0 9.2 %copy.26 = f32[2048,1024]{0,1:T(8,128)} copy(f32[2048,1024]{1,0:T(8,128)} %gather_fusion) | data formatting | bytes 16777216 | tf_op jit(solution)/shard_map/gather | solution.py:57
  56.2 0.0 copy-done.1
  56.2 9.8 %gather_fusion.3 = f32[2048,1024]{1,0:T(8,128)} fusion(f32[64,1024]{1,0:T(8,128)S(1)} %copy-done.1, s32[2048]{0:T(1024)S(1)} %get-tuple-element.11), kind=kCustom, calls=%fused_computation.3 | custom fusion | bytes 16785408 | tf_op jit(solution)/shard_map/gather | solution.py:57
  66.0 0.0 copy-start.2
  66.0 9.2 %copy.29 = f32[2048,1024]{0,1:T(8,128)} copy(f32[2048,1024]{1,0:T(8,128)} %gather_fusion.3) | data formatting | bytes 16777216 | tf_op jit(solution)/shard_map/gather | solution.py:57
  75.2 0.0 all-to-all-done
  75.2 0.5 broadcast.118
  75.7 0.8 reduce.8
  76.5 0.1 reshape.68
  76.6 0.0 copy-done.2
  76.6 5.4 %gather_fusion.1 = f32[1024,1024]{1,0:T(8,128)} fusion(f32[64,1024]{1,0:T(8,128)S(1)} %copy-done.2, s32[1024]{0:T(1024)S(1)} %broadcast_clamp_fusion), kind=kCustom, calls=%fused_computation.1 | custom fusion | bytes 8392704 | tf_op jit(solution)/shard_map/gather | solution.py:45
  82.1 10.2 %all-to-all-start.1 = ((f32[128,8,1024]{2,1,0:T(8,128)}), f32[128,8,1024]{2,1,0:T(8,128)}, u32[]{:S(2)}, u32[]{:S(2)}) async-start(f32[128,8,1024]{2,1,0:T(8,128)} %bitcast.14), calls=%async_computation.1 | async-start | bytes 8388608 | tf_op jit(solution)/shard_map/all_to_all | solution.py:46
  92.3 34.8 %multiply_convert_fusion = (bf16[2048,1024]{1,0:T(8,128)(2,1)S(1)}, bf16[2048,1024]{1,0:T(8,128)(2,1)S(1)}) fusion(f32[2048]{0:T(1024)S(1)} %fusion.39, f32[2048]{0:T(1024)S(1)} %subtract_multiply_fusion), kind=kLoop, calls=%fused_computation.28 | loop fusion | flops 37748736 | bytes 8404992 | tf_op jit(solution)/shard_map/convert.1
  127.0 21.9 %convolution_bitcast_fusion = f32[2048,2048]{0,1:T(8,128)} fusion(bf16[2048,2048]{1,0:T(8,128)(2,1)} %param.8, bf16[2048,1024]{1,0:T(8,128)(2,1)S(1)} %get-tuple-element.9, bf16[2048,1024]{1,0:T(8,128)(2,1)S(1)} %get-tuple-element.10), kind=kOutput, calls=%fused_computation.11 | convolution fusion | flops 17196646400 | bytes 33554432 | tf_op jit(solution)/shard_map/dot_general | solution.py:50
  149.0 0.0 all-to-all-done.1
  149.0 9.8 %all-to-all-start.3 = ((f32[128,1,8]{2,1,0:T(1,128)}), f32[128,1,8]{2,1,0:T(1,128)S(1)}, u32[]{:S(2)}, u32[]{:S(2)}) async-start(f32[128,1,8]{2,1,0:T(1,128)} %bitcast.7), calls=%async_computation.3 | async-start | bytes 131072 | tf_op jit(solution)/shard_map/all_to_all | solution.py:67
  158.8 13.9 %gather_fusion.2 = f32[2048,1024]{1,0:T(8,128)} fusion(f32[1024,1024]{1,0:T(8,128)} %bitcast.4, s32[2048]{0:T(1024)S(1)} %fusion.37), kind=kCustom, calls=%fused_computation.2 | custom fusion | bytes 16785408 | tf_op jit(solution)/shard_map/gather | solution.py:57
  172.6 9.1 %copy.28 = f32[2048,1024]{0,1:T(8,128)} copy(f32[2048,1024]{1,0:T(8,128)} %gather_fusion.2) | data formatting | bytes 16777216 | tf_op jit(solution)/shard_map/gather | solution.py:57
  181.7 19.4 %fusion.9 = f32[2048,1024]{0,1:T(8,128)} fusion(f32[2048,1024]{0,1:T(8,128)} %copy.29, f32[2048,1024]{0,1:T(8,128)} %copy.28, f32[2048,1024]{0,1:T(8,128)} %copy.26, f32[2048,2048]{0,1:T(8,128)} %convolution_bitcast_fusion), kind=kLoop, calls=%fused_computation.22 | loop fusion | flops 16777216 | bytes 50331648 | tf_op jit(solution)/shard_map/sub | solution.py:57
  201.1 9.3 %copy.30 = f32[2048,1024]{1,0:T(8,128)} copy(f32[2048,1024]{0,1:T(8,128)} %fusion.9) | data formatting | bytes 16777216 | tf_op jit(solution)/shard_map/sub | solution.py:57
  210.4 21.2 %scatter_custom_fusion = f32[1024,1024]{1,0:T(8,128)} fusion(s32[2048]{0:T(1024)} %param.11, f32[2048,1024]{1,0:T(8,128)} %copy.30, f32[]{:T(128)} %constant.12.clone.1), kind=kCustom, calls=%fused_computation.36 | custom fusion | flops 2097152 | bytes 4194816 | tf_op jit(solution)/shard_map/scatter-add | solution.py:59
  231.5 0.0 all-to-all-done.3
  231.5 10.2 %all-to-all-start.2 = ((f32[128,8,1024]{2,1,0:T(8,128)}), f32[128,8,1024]{2,1,0:T(8,128)}, u32[]{:S(2)}, u32[]{:S(2)}) async-start(f32[128,8,1024]{2,1,0:T(8,128)} %bitcast.15), calls=%async_computation.2 | async-start | bytes 8388608 | tf_op jit(solution)/shard_map/all_to_all | solution.py:66
  241.7 0.0 all-reduce.3.cloned.1.call-start
  241.8 0.2 convert_reduce_fusion
  242.0 0.1 slice.23
  242.1 103.8 %psum.31 = f32[64]{0:T(128)S(1)} all-reduce(f32[64]{0:T(128)S(1)} %slice.23), channel_id=1, replica_groups=mesh['src'=32,'rcv'=4] {'src','rcv'}, use_global_device_ids=true, to_apply=%region_8.9 | all-reduce | flops 64 | bytes 512 | tf_op jit(solution)/shard_map/psum | solution.py:86
  345.9 0.5 broadcast.119
  346.4 0.8 reduce.9
  347.2 0.1 reshape.134
  347.3 0.1 reshape.116
  347.4 7.8 %scatter_custom_fusion.3 = f32[64]{0:T(128)S(1)} fusion(s32[1024]{0:T(1024)S(1)} %reshape.116, f32[1024]{0:T(1024)S(1)} %reshape.134, f32[]{:T(128)} %constant.13.clone.1), kind=kCustom, calls=%fused_computation.70 | custom fusion | flops 1024 | bytes 260 | tf_op jit(solution)/shard_map/scatter-add | solution.py:73
  355.2 7.2 %fusion.16 = f32[72,1024]{1,0:T(8,128)S(1)} fusion(f32[2048,1024]{0,1:T(8,128)} %fusion.9, s32[2048]{0:T(1024)S(1)} %get-tuple-element.12, s32[2048]{0:T(1024)S(1)} %get-tuple-element.6), kind=kOutput, calls=%fused_computation.33 | convolution fusion | flops 310820864 | bytes 8699904 | tf_op jit(solution)/shard_map/dot_general | solution.py:25
  362.4 4.8 fusion.24
  367.2 0.7 slice.35
  367.9 0.0 all-reduce.3.cloned.1.call-update
  368.0 13.2 %all-reduce = (f32[8,1024]{1,0:T(8,128)S(1)}, f32[8]{0:T(128)S(1)}) all-reduce(f32[8,1024]{1,0:T(8,128)S(1)} %slice.34, f32[8]{0:T(128)S(1)} %bitcast.18), channel_id=1, replica_groups=mesh['src'=32,'rcv'=4] {'rcv'}, use_global_device_ids=true, to_apply=%region_0.1 | all-reduce | flops 8200 | bytes 65600 | tf_op jit(solution)/shard_map/psum | solution.py:85
  381.1 0.7 divide_add_fusion.2
  381.8 125.3 %all-reduce.3.cloned.1.call-done = f32[64,1024]{1,0:T(8,128)} async-done(((f32[64,1024]{1,0:T(8,128)}), f32[64,1024]{1,0:T(8,128)}) %all-reduce.3.cloned.1.call-update) | async-done | bytes 262160 | tf_op jit(solution)/shard_map/psum | solution.py:86
  507.1 1.8 divide_add_fusion
  508.8 0.0 all-to-all-done.2
  508.8 10.1 %scatter_custom_fusion.1 = f32[64,1024]{1,0:T(8,128)S(1)} fusion(s32[1024]{0:T(1024)S(1)} %reshape.116, f32[128,8,1024]{2,1,0:T(8,128)} %all-to-all-done.2, f32[]{:T(128)} %constant.12.clone.1), kind=kCustom, calls=%fused_computation.34 | custom fusion | flops 1048576 | bytes 4456452 | tf_op jit(solution)/shard_map/scatter-add | solution.py:70
  519.0 0.8 divide_add_fusion.1
  (6 shorter events, 0.0 us)
Async XLA Ops:
  7.2 30.0 %copy-start = (f32[8,1024]{1,0:T(8,128)S(1)}, f32[8,1024]{1,0:T(8,128)}, u32[]{:S(2)}) copy-start(f32[8,1024]{1,0:T(8,128)} %param.13) | copy-start | bytes 98308
  8.6 66.6 %all-to-all-start = ((s32[128,1,8]{2,1,0:T(1,128)}), s32[128,1,8]{2,1,0:T(1,128)S(1)}, u32[]{:S(2)}, u32[]{:S(2)}) async-start(s32[128,1,8]{2,1,0:T(1,128)} %bitcast.1), calls=%async_computation | async-start | bytes 131072 | tf_op jit(solution)/shard_map/all_to_all | solution.py:44
  47.0 9.2 %copy-start.1 = (f32[64,1024]{1,0:T(8,128)S(1)}, f32[64,1024]{1,0:T(8,128)}, u32[]{:S(2)}) copy-start(f32[64,1024]{1,0:T(8,128)} %param.15) | copy-start | bytes 786436
  66.0 10.6 %copy-start.2 = (f32[64,1024]{1,0:T(8,128)S(1)}, f32[64,1024]{1,0:T(8,128)}, u32[]{:S(2)}) copy-start(f32[64,1024]{1,0:T(8,128)} %param.14) | copy-start | bytes 786436
  82.1 66.9 %all-to-all-start.1 = ((f32[128,8,1024]{2,1,0:T(8,128)}), f32[128,8,1024]{2,1,0:T(8,128)}, u32[]{:S(2)}, u32[]{:S(2)}) async-start(f32[128,8,1024]{2,1,0:T(8,128)} %bitcast.14), calls=%async_computation.1 | async-start | bytes 8388608 | tf_op jit(solution)/shard_map/all_to_all | solution.py:46
  149.0 82.5 %all-to-all-start.3 = ((f32[128,1,8]{2,1,0:T(1,128)}), f32[128,1,8]{2,1,0:T(1,128)S(1)}, u32[]{:S(2)}, u32[]{:S(2)}) async-start(f32[128,1,8]{2,1,0:T(1,128)} %bitcast.7), calls=%async_computation.3 | async-start | bytes 131072 | tf_op jit(solution)/shard_map/all_to_all | solution.py:67
  231.5 277.3 %all-to-all-start.2 = ((f32[128,8,1024]{2,1,0:T(8,128)}), f32[128,8,1024]{2,1,0:T(8,128)}, u32[]{:S(2)}, u32[]{:S(2)}) async-start(f32[128,8,1024]{2,1,0:T(8,128)} %bitcast.15), calls=%async_computation.2 | async-start | bytes 8388608 | tf_op jit(solution)/shard_map/all_to_all | solution.py:66
  241.7 265.3 %all-reduce.3.cloned.1.call-start = ((), (), s32[]{:S(2)}) async-start(), calls=%async_computation.4 | async-start | bytes 524288 | tf_op jit(solution)/shard_map/psum | solution.py:86
Sparse Core Ops, SparseCore 0:
  368.1 138.9 all-reduce.2
where the time goes:
time: 528 us; the launch traced here: 527 us
  waiting for transfers between devices  125 us (24%)
  blocking collectives  117 us (22%)
  other arithmetic  115 us (22%)
  local copies, waits for them, and re-layouts  79.9 us (15%)
  starting transfers between devices  41.7 us (8%)
  matrix products  33.9 us (6%)
  between operations  14.2 us (3%)
    psum x1, waiting for transfers between devices, local(): off_sum, off_tot = lax.psum((off_part, off_cnt), ('src', 'rcv'))  125 us
    psum x1, blocking collectives, local(): off_sum, off_tot = lax.psum((off_part, off_cnt), ('src', 'rcv'))  104 us
    another operation x1, other arithmetic  34.8 us
    gather x2, local copies, waits for them, and re-layouts, local(): fetched[trace_slot]  23 us
    dot_general x1, matrix products, local(): spectra = jnp.dot(traces, table, preferred_element_type=jnp.float32)  21.9 us
    scatter-add x1, other arithmetic, local(): jax.ops.segment_sum(residual, trace_slot, num_segments=peers * slots)  21.2 us
    sub x1, other arithmetic, local(): logamp - source_terms[src_local] - fetched[trace_slot]  19.4 us
    gather x2, local copies, waits for them, and re-layouts, local(): source_terms[src_local]  19 us
  transfers between devices with their start and end apart: 5, of which 1 were waited for; matrix products, arithmetic and copies ran while one was open for 40% of the time, Pallas kernels for 0%

commit v1 on v0

--- a/solution.py
+++ b/solution.py
@@ -83,7 +83,7 @@
     src_cnt = joint_cnt[:num_src]
     off_cnt = joint_cnt[num_src:]
     src_sum, src_tot = lax.psum((src_part, src_cnt), "rcv")
-    off_sum, off_tot = lax.psum((off_part, off_cnt), ("src", "rcv"))
+    off_sum, off_tot = lax.psum(lax.psum((off_part, off_cnt), "rcv"), "src")
     source_new = source_terms + src_sum / (src_tot + 1.0)[:, None]
     offset_new = offset_terms + off_sum / (off_tot + 1.0)[:, None]
     return (source_new, receiver_new, offset_new)

time: 528 us -> 483 us (0.915)
  waiting for transfers between devices: 125 us -> 98.1 us
  blocking collectives: 117 us -> 99.9 us
    psum x1, blocking collectives: 104 us -> 65.4 us  [local(): off_sum, off_tot = lax.psum(lax.psum((off_part, off_cnt), 'rcv'), 'src')]
    psum x1 -> x2, waiting for transfers between devices: 125 us -> 98 us  [local(): off_sum, off_tot = lax.psum(lax.psum((off_part, off_cnt), 'rcv'), 'src')]
    psum x1, blocking collectives: 13.2 us -> 34.5 us  [local(): src_sum, src_tot = lax.psum((src_part, src_cnt), 'rcv')]
  transfers between devices with their start and end apart: 5 -> 6, of which waited for: 1 -> 1; matrix products, arithmetic and copies ran while one was open for 40% -> 43% of each run, Pallas kernels for 0% -> 0%
where the time goes in v1:
time: 483 us; the launch traced here: 482 us
  other arithmetic  115 us (24%)
  blocking collectives  99.9 us (21%)
  waiting for transfers between devices  98.1 us (20%)
  local copies, waits for them, and re-layouts  79.9 us (17%)
  starting transfers between devices  41.8 us (9%)
  matrix products  33.9 us (7%)
  between operations  14.2 us (3%)
    psum x2, waiting for transfers between devices, local(): off_sum, off_tot = lax.psum(lax.psum((off_part, off_cnt), 'rcv'), 'src')  98 us
    psum x1, blocking collectives, local(): off_sum, off_tot = lax.psum(lax.psum((off_part, off_cnt), 'rcv'), 'src')  65.4 us
    another operation x1, other arithmetic  34.8 us
    psum x1, blocking collectives, local(): src_sum, src_tot = lax.psum((src_part, src_cnt), 'rcv')  34.5 us
    gather x2, local copies, waits for them, and re-layouts, local(): fetched[trace_slot]  23 us
    dot_general x1, matrix products, local(): spectra = jnp.dot(traces, table, preferred_element_type=jnp.float32)  21.9 us
    scatter-add x1, other arithmetic, local(): jax.ops.segment_sum(residual, trace_slot, num_segments=peers * slots)  21.2 us
    sub x1, other arithmetic, local(): logamp - source_terms[src_local] - fetched[trace_slot]  19.4 us
  transfers between devices with their start and end apart: 6, of which 1 were waited for; matrix products, arithmetic and copies ran while one was open for 43% of the time, Pallas kernels for 0%

profile of v1, /device:TPU:1, one launch (start us, length us, event | category | flops | bytes accessed | tf_op | source)
XLA Modules:
  0.0 482.3 jit_solution(6988393943246006110)
XLA Ops:
  7.2 0.0 copy-start
  7.2 1.4 copy.27
  8.6 11.5 %all-to-all-start = ((s32[128,1,8]{2,1,0:T(1,128)}), s32[128,1,8]{2,1,0:T(1,128)S(1)}, u32[]{:S(2)}, u32[]{:S(2)}) async-start(s32[128,1,8]{2,1,0:T(1,128)} %bitcast.1), calls=%async_computation | async-start | bytes 131072 | tf_op jit(solution)/shard_map/all_to_all | solution.py:44
  20.1 0.1 fusion.39
  20.2 0.7 fusion.37
  20.9 0.7 fusion.36
  21.6 0.1 subtract_multiply_fusion
  21.7 14.8 %scatter_custom_fusion.2 = f32[1024]{0:T(1024)S(1)} fusion(s32[2048]{0:T(1024)} %param.11, f32[2048]{0:T(1024)S(1)} %broadcast.70, f32[]{:T(128)} %constant.12.clone.1), kind=kCustom, calls=%fused_computation.67 | custom fusion | flops 2048 | bytes 4608 | tf_op jit(solution)/shard_map/scatter-add | solution.py:62
  36.5 0.7 all_to_all.22
  37.2 0.0 copy-done
  37.2 9.8 %gather_fusion = f32[2048,1024]{1,0:T(8,128)} fusion(f32[8,1024]{1,0:T(8,128)S(1)} %copy-done, s32[2048]{0:T(1024)S(1)} %get-tuple-element.6), kind=kCustom, calls=%fused_computation | custom fusion | bytes 16785408 | tf_op jit(solution)/shard_map/gather | solution.py:57
  47.0 0.0 copy-start.1
  47.0 9.2 %copy.26 = f32[2048,1024]{0,1:T(8,128)} copy(f32[2048,1024]{1,0:T(8,128)} %gather_fusion) | data formatting | bytes 16777216 | tf_op jit(solution)/shard_map/gather | solution.py:57
  56.2 0.0 copy-done.1
  56.2 9.8 %gather_fusion.3 = f32[2048,1024]{1,0:T(8,128)} fusion(f32[64,1024]{1,0:T(8,128)S(1)} %copy-done.1, s32[2048]{0:T(1024)S(1)} %get-tuple-element.12), kind=kCustom, calls=%fused_computation.3 | custom fusion | bytes 16785408 | tf_op jit(solution)/shard_map/gather | solution.py:57
  66.0 0.0 copy-start.2
  66.0 9.2 %copy.29 = f32[2048,1024]{0,1:T(8,128)} copy(f32[2048,1024]{1,0:T(8,128)} %gather_fusion.3) | data formatting | bytes 16777216 | tf_op jit(solution)/shard_map/gather | solution.py:57
  75.2 0.0 all-to-all-done
  75.2 0.5 broadcast.118
  75.7 0.8 reduce.8
  76.5 0.1 reshape.68
  76.6 0.0 copy-done.2
  76.6 5.4 %gather_fusion.1 = f32[1024,1024]{1,0:T(8,128)} fusion(f32[64,1024]{1,0:T(8,128)S(1)} %copy-done.2, s32[1024]{0:T(1024)S(1)} %broadcast_clamp_fusion), kind=kCustom, calls=%fused_computation.1 | custom fusion | bytes 8392704 | tf_op jit(solution)/shard_map/gather | solution.py:45
  82.1 10.2 %all-to-all-start.1 = ((f32[128,8,1024]{2,1,0:T(8,128)}), f32[128,8,1024]{2,1,0:T(8,128)}, u32[]{:S(2)}, u32[]{:S(2)}) async-start(f32[128,8,1024]{2,1,0:T(8,128)} %bitcast.14), calls=%async_computation.1 | async-start | bytes 8388608 | tf_op jit(solution)/shard_map/all_to_all | solution.py:46
  92.3 34.8 %multiply_convert_fusion = (bf16[2048,1024]{1,0:T(8,128)(2,1)S(1)}, bf16[2048,1024]{1,0:T(8,128)(2,1)S(1)}) fusion(f32[2048]{0:T(1024)S(1)} %fusion.39, f32[2048]{0:T(1024)S(1)} %subtract_multiply_fusion), kind=kLoop, calls=%fused_computation.28 | loop fusion | flops 37748736 | bytes 8404992 | tf_op jit(solution)/shard_map/convert.1
  127.0 21.9 %convolution_bitcast_fusion = f32[2048,2048]{0,1:T(8,128)} fusion(bf16[2048,2048]{1,0:T(8,128)(2,1)} %param.8, bf16[2048,1024]{1,0:T(8,128)(2,1)S(1)} %get-tuple-element.10, bf16[2048,1024]{1,0:T(8,128)(2,1)S(1)} %get-tuple-element.11), kind=kOutput, calls=%fused_computation.11 | convolution fusion | flops 17196646400 | bytes 33554432 | tf_op jit(solution)/shard_map/dot_general | solution.py:50
  149.0 0.0 all-to-all-done.1
  149.0 9.8 %all-to-all-start.3 = ((f32[128,1,8]{2,1,0:T(1,128)}), f32[128,1,8]{2,1,0:T(1,128)S(1)}, u32[]{:S(2)}, u32[]{:S(2)}) async-start(f32[128,1,8]{2,1,0:T(1,128)} %bitcast.7), calls=%async_computation.3 | async-start | bytes 131072 | tf_op jit(solution)/shard_map/all_to_all | solution.py:67
  158.8 13.9 %gather_fusion.2 = f32[2048,1024]{1,0:T(8,128)} fusion(f32[1024,1024]{1,0:T(8,128)} %bitcast.4, s32[2048]{0:T(1024)S(1)} %fusion.37), kind=kCustom, calls=%fused_computation.2 | custom fusion | bytes 16785408 | tf_op jit(solution)/shard_map/gather | solution.py:57
  172.6 9.1 %copy.28 = f32[2048,1024]{0,1:T(8,128)} copy(f32[2048,1024]{1,0:T(8,128)} %gather_fusion.2) | data formatting | bytes 16777216 | tf_op jit(solution)/shard_map/gather | solution.py:57
  181.7 19.4 %fusion.9 = f32[2048,1024]{0,1:T(8,128)} fusion(f32[2048,1024]{0,1:T(8,128)} %copy.29, f32[2048,1024]{0,1:T(8,128)} %copy.28, f32[2048,1024]{0,1:T(8,128)} %copy.26, f32[2048,2048]{0,1:T(8,128)} %convolution_bitcast_fusion), kind=kLoop, calls=%fused_computation.22 | loop fusion | flops 16777216 | bytes 50331648 | tf_op jit(solution)/shard_map/sub | solution.py:57
  201.1 9.3 %copy.30 = f32[2048,1024]{1,0:T(8,128)} copy(f32[2048,1024]{0,1:T(8,128)} %fusion.9) | data formatting | bytes 16777216 | tf_op jit(solution)/shard_map/sub | solution.py:57
  210.4 21.2 %scatter_custom_fusion = f32[1024,1024]{1,0:T(8,128)} fusion(s32[2048]{0:T(1024)} %param.11, f32[2048,1024]{1,0:T(8,128)} %copy.30, f32[]{:T(128)} %constant.12.clone.1), kind=kCustom, calls=%fused_computation.36 | custom fusion | flops 2097152 | bytes 4194816 | tf_op jit(solution)/shard_map/scatter-add | solution.py:59
  231.5 0.0 all-to-all-done.3
  231.5 10.2 %all-to-all-start.2 = ((f32[128,8,1024]{2,1,0:T(8,128)}), f32[128,8,1024]{2,1,0:T(8,128)}, u32[]{:S(2)}, u32[]{:S(2)}) async-start(f32[128,8,1024]{2,1,0:T(8,128)} %bitcast.15), calls=%async_computation.2 | async-start | bytes 8388608 | tf_op jit(solution)/shard_map/all_to_all | solution.py:66
  241.7 0.0 all-reduce.4.cloned.1.call-start
  241.8 0.2 convert_reduce_fusion
  242.0 0.1 slice.23
  242.1 0.5 broadcast.119
  242.6 0.8 reduce.9
  243.4 0.1 reshape.134
  243.5 0.1 reshape.116
  243.6 7.8 %scatter_custom_fusion.3 = f32[64]{0:T(128)S(1)} fusion(s32[1024]{0:T(1024)S(1)} %reshape.116, f32[1024]{0:T(1024)S(1)} %reshape.134, f32[]{:T(128)} %constant.13.clone.1), kind=kCustom, calls=%fused_computation.70 | custom fusion | flops 1024 | bytes 260 | tf_op jit(solution)/shard_map/scatter-add | solution.py:73
  251.4 7.2 %fusion.16 = f32[72,1024]{1,0:T(8,128)S(1)} fusion(f32[2048,1024]{0,1:T(8,128)} %fusion.9, s32[2048]{0:T(1024)S(1)} %get-tuple-element.13, s32[2048]{0:T(1024)S(1)} %get-tuple-element.7), kind=kOutput, calls=%fused_computation.33 | convolution fusion | flops 310820864 | bytes 8699904 | tf_op jit(solution)/shard_map/dot_general | solution.py:25
  258.6 4.8 fusion.24
  263.4 0.7 slice.35
  264.1 0.0 all-reduce.4.cloned.1.call-update
  264.1 0.0 all-reduce.6.cloned.1.call-start
  264.2 34.5 %all-reduce = (f32[8,1024]{1,0:T(8,128)S(1)}, f32[8]{0:T(128)S(1)}, f32[64]{0:T(128)S(1)}) all-reduce(f32[8,1024]{1,0:T(8,128)S(1)} %slice.34, f32[8]{0:T(128)S(1)} %bitcast.18, f32[64]{0:T(128)S(1)} %slice.23), channel_id=1, replica_groups=mesh['src'=32,'rcv'=4] {'rcv'}, use_global_device_ids=true, to_apply=%region_0.1 | all-reduce | flops 8264 | bytes 66112 | tf_op jit(solution)/shard_map/psum | solution.py:85
  298.7 65.4 %psum.47 = f32[64]{0:T(128)S(1)} all-reduce(f32[64]{0:T(128)S(1)} %get-tuple-element.5), channel_id=1, replica_groups=mesh['src'=32,'rcv'=4] {'src'}, use_global_device_ids=true, to_apply=%region_10.11 | all-reduce | flops 64 | bytes 512 | tf_op jit(solution)/shard_map/psum | solution.py:86
  364.1 0.7 divide_add_fusion.2
  364.7 0.0 all-reduce.4.cloned.1.call-done
  364.7 0.0 all-reduce.6.cloned.1.call-update
  364.8 98.0 %all-reduce.6.cloned.1.call-done = f32[64,1024]{1,0:T(8,128)} async-done(((f32[64,1024]{1,0:T(8,128)}), f32[64,1024]{1,0:T(8,128)}) %all-reduce.6.cloned.1.call-update) | async-done | bytes 262160 | tf_op jit(solution)/shard_map/psum | solution.py:86
  462.8 1.8 divide_add_fusion
  464.5 0.0 all-to-all-done.2
  464.5 10.1 %scatter_custom_fusion.1 = f32[64,1024]{1,0:T(8,128)S(1)} fusion(s32[1024]{0:T(1024)S(1)} %reshape.116, f32[128,8,1024]{2,1,0:T(8,128)} %all-to-all-done.2, f32[]{:T(128)} %constant.12.clone.1), kind=kCustom, calls=%fused_computation.34 | custom fusion | flops 1048576 | bytes 4456452 | tf_op jit(solution)/shard_map/scatter-add | solution.py:70
  474.7 0.8 divide_add_fusion.1
  (6 shorter events, 0.0 us)
Async XLA Ops:
  7.2 30.0 %copy-start = (f32[8,1024]{1,0:T(8,128)S(1)}, f32[8,1024]{1,0:T(8,128)}, u32[]{:S(2)}) copy-start(f32[8,1024]{1,0:T(8,128)} %param.13) | copy-start | bytes 98308
  8.6 66.6 %all-to-all-start = ((s32[128,1,8]{2,1,0:T(1,128)}), s32[128,1,8]{2,1,0:T(1,128)S(1)}, u32[]{:S(2)}, u32[]{:S(2)}) async-start(s32[128,1,8]{2,1,0:T(1,128)} %bitcast.1), calls=%async_computation | async-start | bytes 131072 | tf_op jit(solution)/shard_map/all_to_all | solution.py:44
  47.0 9.2 %copy-start.1 = (f32[64,1024]{1,0:T(8,128)S(1)}, f32[64,1024]{1,0:T(8,128)}, u32[]{:S(2)}) copy-start(f32[64,1024]{1,0:T(8,128)} %param.15) | copy-start | bytes 786436
  66.0 10.6 %copy-start.2 = (f32[64,1024]{1,0:T(8,128)S(1)}, f32[64,1024]{1,0:T(8,128)}, u32[]{:S(2)}) copy-start(f32[64,1024]{1,0:T(8,128)} %param.14) | copy-start | bytes 786436
  82.1 66.9 %all-to-all-start.1 = ((f32[128,8,1024]{2,1,0:T(8,128)}), f32[128,8,1024]{2,1,0:T(8,128)}, u32[]{:S(2)}, u32[]{:S(2)}) async-start(f32[128,8,1024]{2,1,0:T(8,128)} %bitcast.14), calls=%async_computation.1 | async-start | bytes 8388608 | tf_op jit(solution)/shard_map/all_to_all | solution.py:46
  149.0 82.5 %all-to-all-start.3 = ((f32[128,1,8]{2,1,0:T(1,128)}), f32[128,1,8]{2,1,0:T(1,128)S(1)}, u32[]{:S(2)}, u32[]{:S(2)}) async-start(f32[128,1,8]{2,1,0:T(1,128)} %bitcast.7), calls=%async_computation.3 | async-start | bytes 131072 | tf_op jit(solution)/shard_map/all_to_all | solution.py:67
  231.5 233.0 %all-to-all-start.2 = ((f32[128,8,1024]{2,1,0:T(8,128)}), f32[128,8,1024]{2,1,0:T(8,128)}, u32[]{:S(2)}, u32[]{:S(2)}) async-start(f32[128,8,1024]{2,1,0:T(8,128)} %bitcast.15), calls=%async_computation.2 | async-start | bytes 8388608 | tf_op jit(solution)/shard_map/all_to_all | solution.py:66
  241.7 123.0 %all-reduce.4.cloned.1.call-start = ((), (), s32[]{:S(2)}) async-start(), calls=%async_computation.4 | async-start | bytes 524288 | tf_op jit(solution)/shard_map/psum | solution.py:86
  264.1 198.7 %all-reduce.6.cloned.1.call-start = ((), (), s32[]{:S(2)}) async-start(), calls=%async_computation.5 | async-start | bytes 524288 | tf_op jit(solution)/shard_map/psum | solution.py:86
Sparse Core Ops, SparseCore 0:
  264.2 43.2 all-reduce.3
  364.9 97.8 all-reduce.5
